TPU v7x, 32 devices: a whole 2x2x4 slice. The times are simulated.
32 devices in a mesh: group: 2 (over x), col: 16 (over z, y, core).
Axes of the slice: x: 2, y: 2, z: 4, core: 2. Of those that a mesh axis runs over, the one named last changes fastest.
Arguments:
- homolog_embedding: bfloat16 [192, 64, 256], P('group', 'col'), parts along dimension 0, may hold values from -6 to 6
- left_factor_matrix: bfloat16 [256, 32], replicated, may hold values from -0.375 to 0.375
- right_factor_matrix: bfloat16 [256, 32], replicated, may hold values from -0.375 to 0.375
- decoder: bfloat16 [1024, 128], replicated, may hold values from -2 to 2
- pair_output_bias: float32 [128], replicated, may hold values from -3 to 3
- pair_output_gradient: bfloat16 [128, 64, 128], P('group', 'col'), parts along dimension 0, may hold values from -6 to 6
Outputs:
- first_operand_gradient: float32 [192, 64, 32], P('group', 'col'), parts along dimension 0
- second_operand_gradient: float32 [192, 64, 32], P('group', 'col'), parts along dimension 0
- alignment_gradient: bfloat16 [192, 64, 256], P('group', 'col'), parts along dimension 0
There are 2 independent parts, one for each index of `group`. A program takes and returns all parts, laid end to end along the dimension named above; an argument that names none is the same for every part. Nothing has to cross between parts.
All inputs are finite; a program needn't handle non-finite values.
Results may differ from a plain program's by a relative error of at most 0.0083.
Values may be sent and summed in bfloat16 or wider, within the bound.
A program may use at most 64 MiB of HBM per device.

v0:
```python
import jax
import jax.numpy as jnp
from jax import lax
from jax.sharding import PartitionSpec as P


def per_device(
    homolog_embedding,
    left_factor_matrix,
    right_factor_matrix,
    decoder,
    pair_output_bias,
    pair_output_gradient,
):
    alignment_row_count, local_residue_start, alignment_channel_width = homolog_embedding.shape
    operand_channel_width = left_factor_matrix.shape[1]
    channels = decoder.shape[1]
    residue_total_count = local_residue_start * lax.axis_size("col")
    reciprocal_rows = 1.0 / alignment_row_count
    block_res = local_residue_start * max(1, 96 // local_residue_start)
    alignment_flattened_rows = homolog_embedding.reshape(
        alignment_row_count * local_residue_start, alignment_channel_width
    )
    first_operand_rows = (
        jnp.dot(alignment_flattened_rows, left_factor_matrix, preferred_element_type=jnp.float32)
        .astype(jnp.bfloat16)
        .reshape(alignment_row_count, local_residue_start * operand_channel_width)
    )
    second_operand_rows = (
        jnp.dot(alignment_flattened_rows, right_factor_matrix, preferred_element_type=jnp.float32)
        .astype(jnp.bfloat16)
        .reshape(alignment_row_count, local_residue_start * operand_channel_width)
    )
    second_operand_local = second_operand_rows.reshape(
        alignment_row_count, local_residue_start, operand_channel_width
    )

    def outer_slopes(slope_rows, rows_by_length, col_span):
        backward = (
            jnp.dot(slope_rows, decoder.T, preferred_element_type=jnp.float32) * reciprocal_rows
        )
        return backward.astype(jnp.bfloat16).reshape(
            rows_by_length, col_span, operand_channel_width, operand_channel_width
        )

    offset_col = jnp.int32(0)
    second_operand_gradient = jnp.zeros(
        (alignment_row_count, local_residue_start, operand_channel_width), jnp.float32
    )
    stored = jnp.zeros((residue_total_count, local_residue_start * channels), jnp.bfloat16)
    left_segment = lax.all_gather(first_operand_rows, "col", axis=1, tiled=True)
    right_segment = lax.all_gather(second_operand_rows, "col", axis=1, tiled=True)
    right_whole = right_segment
    piece_res = left_segment.shape[1] // operand_channel_width
    first_res = offset_col // operand_channel_width
    collected = []
    for split_offset in range(0, piece_res, block_res):
        split_rows_by_length = min(block_res, piece_res - split_offset)
        split_left_block = left_segment[
            :,
            split_offset
            * operand_channel_width : (split_offset + split_rows_by_length)
            * operand_channel_width,
        ].reshape(alignment_row_count, split_rows_by_length, operand_channel_width)
        collected.append((split_rows_by_length, split_left_block, first_res + split_offset))
    for rows_by_length, left_block, first_row in collected:
        products = (
            jnp.einsum(
                "sic,sjd->ijcd",
                left_block,
                second_operand_local,
                preferred_element_type=jnp.float32,
            )
            * reciprocal_rows
        )
        products = products.astype(jnp.bfloat16).reshape(
            rows_by_length * local_residue_start, operand_channel_width * operand_channel_width
        )
        linear = jnp.dot(products, decoder, preferred_element_type=jnp.float32) + pair_output_bias
        upstream = lax.dynamic_slice_in_dim(pair_output_gradient, first_row, rows_by_length, 0)
        upstream = upstream.reshape(rows_by_length * local_residue_start, channels).astype(
            jnp.float32
        )
        accumulate_slope_rows = (upstream * 2.0 * jnp.maximum(linear, 0.0)).astype(jnp.bfloat16)
        stored = lax.dynamic_update_slice_in_dim(
            stored,
            accumulate_slope_rows.reshape(rows_by_length, local_residue_start * channels),
            first_row,
            0,
        )
        accumulate_slopes = outer_slopes(accumulate_slope_rows, rows_by_length, local_residue_start)
        second_operand_gradient = second_operand_gradient + jnp.einsum(
            "ijcd,sic->sjd", accumulate_slopes, left_block, preferred_element_type=jnp.float32
        )
    second_operand_gradient, stored, right_whole = (second_operand_gradient, stored, right_whole)
    received = lax.all_to_all(stored, "col", split_axis=0, concat_axis=1, tiled=True)
    right_all = right_whole.reshape(alignment_row_count, residue_total_count, operand_channel_width)
    col_span = local_residue_start * max(
        max(1, 96 // local_residue_start), lax.axis_size("col") // 8
    )
    first_operand_gradient = jnp.zeros(
        (alignment_row_count, local_residue_start, operand_channel_width), jnp.float32
    )
    for offset in range(0, residue_total_count, col_span):
        width_cols = min(col_span, residue_total_count - offset)
        slope_rows = received[:, offset * channels : (offset + width_cols) * channels].reshape(
            local_residue_start * width_cols, channels
        )
        slopes = outer_slopes(slope_rows, local_residue_start, width_cols)
        first_operand_gradient = first_operand_gradient + jnp.einsum(
            "ijcd,sjd->sic",
            slopes,
            right_all[:, offset : offset + width_cols],
            preferred_element_type=jnp.float32,
        )
    first_operand_gradient_step = first_operand_gradient.astype(jnp.bfloat16).reshape(
        alignment_row_count * local_residue_start, operand_channel_width
    )
    second_operand_gradient_step = second_operand_gradient.astype(jnp.bfloat16).reshape(
        alignment_row_count * local_residue_start, operand_channel_width
    )
    alignment_gradient = jnp.dot(
        first_operand_gradient_step, left_factor_matrix.T, preferred_element_type=jnp.float32
    ) + jnp.dot(
        second_operand_gradient_step, right_factor_matrix.T, preferred_element_type=jnp.float32
    )
    alignment_gradient = alignment_gradient.astype(jnp.bfloat16).reshape(
        alignment_row_count, local_residue_start, alignment_channel_width
    )
    return (first_operand_gradient, second_operand_gradient, alignment_gradient)


def solution(mesh):
    placed = (P("group", "col", None), P(), P(), P(), P(), P("group", "col", None))
    return jax.shard_map(
        per_device,
        mesh=mesh,
        in_specs=placed,
        out_specs=(P("group", "col", None), P("group", "col", None), P("group", "col", None)),
        check_vma=False,
    )
```

profile of v0, /device:TPU:0, one launch (start us, length us, event | category | flops | bytes accessed | tf_op | source)
XLA Modules:
  0.0 74.2 jit_solution(9161705522396213601)
XLA Ops:
  0.6 0.0 copy-start
  0.7 1.0 %reshape.53 = bf16[384,256]{1,0:T(8,128)(2,1)S(1)} reshape(bf16[96,4,256]{2,1,0:T(4,128)(2,1)} %param.6) | data formatting | bytes 393216 | tf_op jit(solution)/shard_map/reshape | solution.py:21
  1.7 0.9 %convolution_convert_fusion = bf16[384,32]{0,1:T(8,128)(2,1)S(1)} fusion(bf16[384,256]{1,0:T(8,128)(2,1)S(1)} %reshape.53, bf16[256,32]{0,1:T(8,128)(2,1)} %param.7), kind=kOutput, calls=%fused_computation.14 | convolution fusion | flops 6303744 | bytes 237568 | tf_op jit(solution)/shard_map/dot_general | solution.py:25
  2.6 0.1 copy.31
  2.7 0.1 reshape.56
  2.8 24.2 %all_gather.7 = bf16[96,2048]{1,0:T(8,128)(2,1)S(1)} all-gather(bf16[96,128]{1,0:T(8,128)(2,1)S(1)} %reshape.56), channel_id=1, replica_groups=mesh['group'=2,'col'=16] {'col'}, dimensions={1}, use_global_device_ids=true | all-gather | bytes 417792 | tf_op jit(solution)/shard_map/all_gather | solution.py:51
  27.0 0.3 copy.32
  27.3 0.2 convolution_convert_fusion.1
  27.5 0.1 copy.28
  27.6 1.6 %fusion = bf16[64,4,32,32]{0,3,2,1:T(8,128)(2,1)} fusion(bf16[96,64,32]{0,2,1:T(8,128)(2,1)S(1)} %bitcast.48, bf16[96,4,32,1]{2,1,0,3:T(4,128)(2,1)S(1)} %bitcast.51), kind=kOutput, calls=%fused_computation.1 | convolution fusion | flops 50855936 | bytes 942080 | tf_op jit(solution)/shard_map/sic,sjd->ijcd/dot_general | solution.py:68
  29.3 4.2 %copy.35 = bf16[64,4,32,32]{3,2,1,0:T(8,128)(2,1)S(1)} copy(bf16[64,4,32,32]{0,3,2,1:T(8,128)(2,1)} %fusion) | data formatting | bytes 1048576 | tf_op jit(solution)/shard_map/convert_element_type | solution.py:76
  33.5 2.2 %reshape.58 = bf16[256,1024]{1,0:T(8,128)(2,1)S(1)} reshape(bf16[64,4,32,32]{3,2,1,0:T(8,128)(2,1)S(1)} %copy.35) | data formatting | bytes 1048576 | tf_op jit(solution)/shard_map/reshape | solution.py:76
  35.7 0.9 %convert_multiply_fusion = f32[64,4,128]{2,1,0:T(4,128)S(1)} fusion(bf16[64,4,128]{2,1,0:T(4,128)(2,1)} %param.11), kind=kLoop, calls=%fused_computation.18 | loop fusion | flops 65536 | bytes 196608 | tf_op jit(solution)/shard_map/mul | solution.py:84
  36.6 0.3 fusion.6
  36.9 0.7 all_to_all.12
  37.6 4.2 %all-to-all-start = ((bf16[16,4,512]{2,1,0:T(4,128)(2,1)}), bf16[16,4,512]{2,1,0:T(4,128)(2,1)}, u32[]{:S(2)}, u32[]{:S(2)}) async-start(bf16[16,4,512]{2,1,0:T(4,128)(2,1)} %all_to_all.12), calls=%async_computation | async-start | bytes 131072 | tf_op jit(solution)/shard_map/all_to_all | solution.py:96
  41.7 0.7 reshape.54
  42.5 0.3 fusion.2
  42.8 1.6 %reshape.61 = bf16[64,4,32,32]{3,2,1,0:T(8,128)(2,1)S(1)} reshape(bf16[256,1024]{1,0:T(8,128)(2,1)S(1)} %fusion.2) | data formatting | bytes 1048576 | tf_op jit(solution)/shard_map/reshape | solution.py:42
  44.4 1.3 %fusion.11 = (bf16[96,4,32]{0,2,1:T(8,128)(2,1)S(1)}, f32[96,4,32]{0,2,1:T(8,128)}) fusion(bf16[96,64,32,1]{0,2,3,1:T(8,128)(2,1)S(1)} %bitcast.49, bf16[64,4,32,32]{3,2,1,0:T(8,128)(2,1)S(1)} %reshape.61), kind=kOutput, calls=%fused_computation.21 | convolution fusion | flops 50343936 | bytes 991232 | tf_op jit(solution)/shard_map/ijcd,sic->sjd/dot_general | solution.py:92
  45.7 22.7 %all_gather.6 = bf16[96,2048]{1,0:T(8,128)(2,1)S(1)} all-gather(bf16[96,128]{1,0:T(8,128)(2,1)S(1)} %copy-done.1), channel_id=1, replica_groups=mesh['group'=2,'col'=16] {'col'}, dimensions={1}, use_global_device_ids=true | all-gather | bytes 417792 | tf_op jit(solution)/shard_map/all_gather | solution.py:52
  68.4 0.3 copy.29
  68.7 0.1 copy.41
  68.8 0.9 %copy.36 = bf16[4,16,512]{2,1,0:T(8,128)(2,1)S(1)} copy(bf16[4,16,512]{2,0,1:T(4,128)(2,1)} %bitcast.8) | data formatting | bytes 131072 | tf_op jit(solution)/shard_map/all_to_all | solution.py:96
  69.7 0.1 reshape.59
  69.7 0.3 fusion.1
  70.0 1.6 %reshape.71 = bf16[4,64,32,32]{3,2,1,0:T(8,128)(2,1)S(1)} reshape(bf16[256,1024]{1,0:T(8,128)(2,1)S(1)} %fusion.1) | data formatting | bytes 1048576 | tf_op jit(solution)/shard_map/reshape | solution.py:42
  71.6 1.3 %fusion.10 = (bf16[96,4,32]{0,2,1:T(8,128)(2,1)S(1)}, f32[96,4,32]{0,2,1:T(8,128)}) fusion(bf16[96,64,32,1]{0,2,1,3:T(8,128)(2,1)S(1)} %bitcast.50, bf16[4,64,32,32]{3,2,1,0:T(8,128)(2,1)S(1)} %reshape.71), kind=kOutput, calls=%fused_computation.20 | convolution fusion | flops 50343936 | bytes 991232 | tf_op jit(solution)/shard_map/ijcd,sjd->sic/dot_general | solution.py:110
  73.0 0.1 copy.40
  73.1 0.2 fusion.12
  73.3 0.2 fusion.3
  73.5 0.7 reshape.64
  (10 shorter events, 0.0 us)
Async XLA Ops:
  0.6 36.0 %copy-start = (bf16[1024,128]{1,0:T(8,128)(2,1)S(1)}, bf16[1024,128]{1,0:T(8,128)(2,1)}, u32[]{:S(2)}) copy-start(bf16[1024,128]{1,0:T(8,128)(2,1)} %param.9) | copy-start | bytes 786436
  0.6 26.7 %copy-start.3 = (bf16[256,32]{0,1:T(8,128)(2,1)S(1)}, bf16[256,32]{0,1:T(8,128)(2,1)}, u32[]{:S(2)}) copy-start(bf16[256,32]{0,1:T(8,128)(2,1)} %param.8) | copy-start | bytes 49156
  33.5 3.1 %copy-start.4 = (f32[128]{0:T(128)S(1)}, f32[128]{0:T(128)}, u32[]{:S(2)}) copy-start(f32[128]{0:T(128)} %param.10) | copy-start | bytes 1540
  37.6 31.2 %all-to-all-start = ((bf16[16,4,512]{2,1,0:T(4,128)(2,1)}), bf16[16,4,512]{2,1,0:T(4,128)(2,1)}, u32[]{:S(2)}, u32[]{:S(2)}) async-start(bf16[16,4,512]{2,1,0:T(4,128)(2,1)} %all_to_all.12), calls=%async_computation | async-start | bytes 131072 | tf_op jit(solution)/shard_map/all_to_all | solution.py:96
  42.8 3.0 %copy-start.1 = (bf16[96,128]{1,0:T(8,128)(2,1)S(1)}, bf16[96,128]{1,0:T(8,128)(2,1)}, u32[]{:S(2)}) copy-start(bf16[96,128]{1,0:T(8,128)(2,1)} %reshape.54) | copy-start | bytes 73732
  70.0 3.1 %copy-start.2 = (bf16[256,32]{0,1:T(8,128)(2,1)S(1)}, bf16[256,32]{0,1:T(8,128)(2,1)}, u32[]{:S(2)}) copy-start(bf16[256,32]{0,1:T(8,128)(2,1)} %param.7) | copy-start | bytes 49156
where the time goes:
time: 74.6 us; the launch traced here: 74.2 us
  blocking collectives  46.9 us (63%)
  local copies, waits for them, and re-layouts  14.9 us (20%)
  matrix products  6.57 us (9%)
  starting transfers between devices  4.16 us (6%)
  other arithmetic  0.87 us (1%)
  between operations  0.86 us (1%)
    all_gather x1, blocking collectives, per_device(): left_segment = lax.all_gather(first_operand_rows, 'col', axis=1, tiled=True)  24.2 us
    all_gather x1, blocking collectives, per_device(): lax.all_gather(second_operand_rows, 'col', axis=1, tiled=True)  22.7 us
    convert_element_type x1, local copies, waits for them, and re-layouts, per_device(): products.astype(jnp.bfloat16)  4.19 us
    all_to_all x1, starting transfers between devices, per_device(): lax.all_to_all(stored, 'col', split_axis=0, concat_axis=1, tiled=True)  4.16 us
    reshape x2, local copies, waits for them, and re-layouts, outer_slopes(): backward.astype(jnp.bfloat16)  3.16 us
    reshape x1, local copies, waits for them, and re-layouts, per_device(): products.astype(jnp.bfloat16)  2.23 us
    dot_general x1, matrix products, per_device(): jnp.einsum('sic,sjd->ijcd', left_block, second_operand_local, preferred_e...  1.63 us
    all_to_all x2, local copies, waits for them, and re-layouts, per_device(): lax.all_to_all(stored, 'col', split_axis=0, concat_axis=1, tiled=True)  1.52 us
  transfers between devices with their start and end apart: 1, of which 0 were waited for; matrix products, arithmetic and copies ran while one was open for 6% of the time, Pallas kernels for 0%

commit v1 on v0

--- a/solution.py
+++ b/solution.py
@@ -48,7 +48,7 @@
         (alignment_row_count, local_residue_start, operand_channel_width), jnp.float32
     )
     stored = jnp.zeros((residue_total_count, local_residue_start * channels), jnp.bfloat16)
-    left_segment = lax.all_gather(first_operand_rows, "col", axis=1, tiled=True)
+    left_segment = jnp.concatenate(lax.all_gather(first_operand_rows, "col"), axis=1)
     right_segment = lax.all_gather(second_operand_rows, "col", axis=1, tiled=True)
     right_whole = right_segment
     piece_res = left_segment.shape[1] // operand_channel_width

time: 74.6 us -> 74.6 us (level)
  no operation moved by 1% of the time
where the time goes in v1:
time: 74.6 us; the launch traced here: 74.2 us
  blocking collectives  46.9 us (63%)
  local copies, waits for them, and re-layouts  14.9 us (20%)
  matrix products  6.57 us (9%)
  starting transfers between devices  4.16 us (6%)
  other arithmetic  0.87 us (1%)
  between operations  0.85 us (1%)
    all_gather x1, blocking collectives, per_device(): lax.all_gather(first_operand_rows, 'col')  24.2 us
    all_gather x1, blocking collectives, per_device(): lax.all_gather(second_operand_rows, 'col', axis=1, tiled=True)  22.7 us
    convert_element_type x1, local copies, waits for them, and re-layouts, per_device(): products.astype(jnp.bfloat16)  4.19 us
    all_to_all x1, starting transfers between devices, per_device(): lax.all_to_all(stored, 'col', split_axis=0, concat_axis=1, tiled=True)  4.16 us
    reshape x2, local copies, waits for them, and re-layouts, outer_slopes(): backward.astype(jnp.bfloat16)  3.16 us
    reshape x1, local copies, waits for them, and re-layouts, per_device(): products.astype(jnp.bfloat16)  2.23 us
    dot_general x1, matrix products, per_device(): jnp.einsum('sic,sjd->ijcd', left_block, second_operand_local, preferred_e...  1.63 us
    all_to_all x2, local copies, waits for them, and re-layouts, per_device(): lax.all_to_all(stored, 'col', split_axis=0, concat_axis=1, tiled=True)  1.52 us
  transfers between devices with their start and end apart: 1, of which 0 were waited for; matrix products, arithmetic and copies ran while one was open for 6% of the time, Pallas kernels for 0%

profile of v1, /device:TPU:0, one launch (start us, length us, event | category | flops | bytes accessed | tf_op | source)
XLA Modules:
  0.0 74.2 jit_solution(1012123003351371016)
XLA Ops:
  0.6 0.0 copy-start
  0.7 1.0 %reshape.50 = bf16[384,256]{1,0:T(8,128)(2,1)S(1)} reshape(bf16[96,4,256]{2,1,0:T(4,128)(2,1)} %param.6) | data formatting | bytes 393216 | tf_op jit(solution)/shard_map/reshape | solution.py:21
  1.7 0.9 %convolution_convert_fusion = bf16[384,32]{0,1:T(8,128)(2,1)S(1)} fusion(bf16[384,256]{1,0:T(8,128)(2,1)S(1)} %reshape.50, bf16[256,32]{0,1:T(8,128)(2,1)} %param.7), kind=kOutput, calls=%fused_computation.14 | convolution fusion | flops 6303744 | bytes 237568 | tf_op jit(solution)/shard_map/dot_general | solution.py:25
  2.6 0.1 copy.31
  2.7 0.1 all_gather_reshape.3
  2.8 24.2 %all_gather.7 = bf16[16,96,128]{2,1,0:T(8,128)(2,1)S(1)} all-gather(bf16[1,96,128]{2,1,0:T(8,128)(2,1)S(1)} %all_gather_reshape.3), channel_id=1, replica_groups=mesh['group'=2,'col'=16] {'col'}, dimensions={0}, use_global_device_ids=true | all-gather | bytes 417792 | tf_op jit(solution)/shard_map/all_gather | solution.py:51
  27.0 0.3 copy.32
  27.3 0.2 convolution_convert_fusion.1
  27.5 0.1 copy.28
  27.6 1.6 %fusion = bf16[64,4,32,32]{0,3,2,1:T(8,128)(2,1)} fusion(bf16[96,64,32]{0,2,1:T(8,128)(2,1)S(1)} %bitcast.50, bf16[96,4,32,1]{2,1,0,3:T(4,128)(2,1)S(1)} %bitcast.53), kind=kOutput, calls=%fused_computation.1 | convolution fusion | flops 50855936 | bytes 942080 | tf_op jit(solution)/shard_map/sic,sjd->ijcd/dot_general | solution.py:68
  29.3 4.2 %copy.35 = bf16[64,4,32,32]{3,2,1,0:T(8,128)(2,1)S(1)} copy(bf16[64,4,32,32]{0,3,2,1:T(8,128)(2,1)} %fusion) | data formatting | bytes 1048576 | tf_op jit(solution)/shard_map/convert_element_type | solution.py:76
  33.5 2.2 %reshape.54 = bf16[256,1024]{1,0:T(8,128)(2,1)S(1)} reshape(bf16[64,4,32,32]{3,2,1,0:T(8,128)(2,1)S(1)} %copy.35) | data formatting | bytes 1048576 | tf_op jit(solution)/shard_map/reshape | solution.py:76
  35.7 0.9 %convert_multiply_fusion = f32[64,4,128]{2,1,0:T(4,128)S(1)} fusion(bf16[64,4,128]{2,1,0:T(4,128)(2,1)} %param.11), kind=kLoop, calls=%fused_computation.18 | loop fusion | flops 65536 | bytes 196608 | tf_op jit(solution)/shard_map/mul | solution.py:84
  36.6 0.3 fusion.6
  36.9 0.7 all_to_all.12
  37.6 4.2 %all-to-all-start = ((bf16[16,4,512]{2,1,0:T(4,128)(2,1)}), bf16[16,4,512]{2,1,0:T(4,128)(2,1)}, u32[]{:S(2)}, u32[]{:S(2)}) async-start(bf16[16,4,512]{2,1,0:T(4,128)(2,1)} %all_to_all.12), calls=%async_computation | async-start | bytes 131072 | tf_op jit(solution)/shard_map/all_to_all | solution.py:96
  41.7 0.7 reshape.51
  42.5 0.3 fusion.2
  42.8 1.6 %reshape.57 = bf16[64,4,32,32]{3,2,1,0:T(8,128)(2,1)S(1)} reshape(bf16[256,1024]{1,0:T(8,128)(2,1)S(1)} %fusion.2) | data formatting | bytes 1048576 | tf_op jit(solution)/shard_map/reshape | solution.py:42
  44.4 1.3 %fusion.11 = (bf16[96,4,32]{0,2,1:T(8,128)(2,1)S(1)}, f32[96,4,32]{0,2,1:T(8,128)}) fusion(bf16[96,64,32,1]{0,2,3,1:T(8,128)(2,1)S(1)} %bitcast.51, bf16[64,4,32,32]{3,2,1,0:T(8,128)(2,1)S(1)} %reshape.57), kind=kOutput, calls=%fused_computation.21 | convolution fusion | flops 50343936 | bytes 991232 | tf_op jit(solution)/shard_map/ijcd,sic->sjd/dot_general | solution.py:92
  45.7 22.7 %all_gather.6 = bf16[96,2048]{1,0:T(8,128)(2,1)S(1)} all-gather(bf16[96,128]{1,0:T(8,128)(2,1)S(1)} %copy-done.1), channel_id=1, replica_groups=mesh['group'=2,'col'=16] {'col'}, dimensions={1}, use_global_device_ids=true | all-gather | bytes 417792 | tf_op jit(solution)/shard_map/all_gather | solution.py:52
  68.4 0.3 copy.29
  68.7 0.1 copy.41
  68.8 0.9 %copy.36 = bf16[4,16,512]{2,1,0:T(8,128)(2,1)S(1)} copy(bf16[4,16,512]{2,0,1:T(4,128)(2,1)} %bitcast.9) | data formatting | bytes 131072 | tf_op jit(solution)/shard_map/all_to_all | solution.py:96
  69.7 0.1 reshape.55
  69.7 0.3 fusion.1
  70.0 1.6 %reshape.67 = bf16[4,64,32,32]{3,2,1,0:T(8,128)(2,1)S(1)} reshape(bf16[256,1024]{1,0:T(8,128)(2,1)S(1)} %fusion.1) | data formatting | bytes 1048576 | tf_op jit(solution)/shard_map/reshape | solution.py:42
  71.6 1.3 %fusion.10 = (bf16[96,4,32]{0,2,1:T(8,128)(2,1)S(1)}, f32[96,4,32]{0,2,1:T(8,128)}) fusion(bf16[96,64,32,1]{0,2,1,3:T(8,128)(2,1)S(1)} %bitcast.52, bf16[4,64,32,32]{3,2,1,0:T(8,128)(2,1)S(1)} %reshape.67), kind=kOutput, calls=%fused_computation.20 | convolution fusion | flops 50343936 | bytes 991232 | tf_op jit(solution)/shard_map/ijcd,sjd->sic/dot_general | solution.py:110
  73.0 0.1 copy.40
  73.1 0.2 fusion.12
  73.3 0.2 fusion.3
  73.5 0.7 reshape.60
  (10 shorter events, 0.0 us)
Async XLA Ops:
  0.6 36.0 %copy-start = (bf16[1024,128]{1,0:T(8,128)(2,1)S(1)}, bf16[1024,128]{1,0:T(8,128)(2,1)}, u32[]{:S(2)}) copy-start(bf16[1024,128]{1,0:T(8,128)(2,1)} %param.9) | copy-start | bytes 786436
  0.6 26.7 %copy-start.3 = (bf16[256,32]{0,1:T(8,128)(2,1)S(1)}, bf16[256,32]{0,1:T(8,128)(2,1)}, u32[]{:S(2)}) copy-start(bf16[256,32]{0,1:T(8,128)(2,1)} %param.8) | copy-start | bytes 49156
  33.5 3.1 %copy-start.4 = (f32[128]{0:T(128)S(1)}, f32[128]{0:T(128)}, u32[]{:S(2)}) copy-start(f32[128]{0:T(128)} %param.10) | copy-start | bytes 1540
  37.6 31.2 %all-to-all-start = ((bf16[16,4,512]{2,1,0:T(4,128)(2,1)}), bf16[16,4,512]{2,1,0:T(4,128)(2,1)}, u32[]{:S(2)}, u32[]{:S(2)}) async-start(bf16[16,4,512]{2,1,0:T(4,128)(2,1)} %all_to_all.12), calls=%async_computation | async-start | bytes 131072 | tf_op jit(solution)/shard_map/all_to_all | solution.py:96
  42.8 3.0 %copy-start.1 = (bf16[96,128]{1,0:T(8,128)(2,1)S(1)}, bf16[96,128]{1,0:T(8,128)(2,1)}, u32[]{:S(2)}) copy-start(bf16[96,128]{1,0:T(8,128)(2,1)} %reshape.51) | copy-start | bytes 73732
  70.0 3.1 %copy-start.2 = (bf16[256,32]{0,1:T(8,128)(2,1)S(1)}, bf16[256,32]{0,1:T(8,128)(2,1)}, u32[]{:S(2)}) copy-start(bf16[256,32]{0,1:T(8,128)(2,1)} %param.7) | copy-start | bytes 49156
